TPU v7x, 32 devices: a whole 2x2x4 slice. The times are simulated.
32 devices in a mesh: branch: 2 (over core), seq: 4 (over z), head: 4 (over y, x).
Axes of the slice: x: 2, y: 2, z: 4, core: 2. Of those that a mesh axis runs over, the one named last changes fastest.
Arguments:
- tokens: bfloat16 [1024, 3072], P('seq', 'head'), may hold values from -10 to 10
- valid_counts: int32 [4], P('seq'), may hold values from 1 to 256, 768 in all
- shared_qkv: bfloat16 [3072, 3, 1536], P('branch', None, 'head'), may hold values from -0.08479832 to 0.08479832
- shared_out: bfloat16 [1536, 3072], P('head', 'branch'), may hold values from -0.15625 to 0.15625
- skipped_qkv: bfloat16 [3072, 3, 1536], P('branch', None, 'head'), may hold values from -0.08479832 to 0.08479832
- skipped_out: bfloat16 [1536, 3072], P('head', 'branch'), may hold values from -0.15625 to 0.15625
- modulation: float32 [2, 3, 3072], replicated, may hold values from -3 to 3
- qk_gains: float32 [2, 2, 128], replicated, may hold values from 1.2 to 5.5
Outputs:
- branches: bfloat16 [2, 1024, 3072], P('branch', 'seq', 'head')
Inputs may be any that keep to these rules, and one draw needn't show every extreme that they name: `valid_counts`: each entry counts the leading real tokens of one shard of 256 slots; the rest are padding. The entries sum to 768 and one of them equals 256.
All inputs are finite; a program needn't handle non-finite values.
Results may differ from a plain program's by a relative error of at most 0.01.
Values may be sent and summed in bfloat16 or wider, within the bound.
No kernel may reach another device: no remote copies, remote signals or barrier semaphores. Data moves between devices by JAX's collectives and lax.ppermute only.
A program may use at most 128 MiB of HBM per device.

v0:
```python
import jax
import jax.numpy as jnp
from jax import lax
from jax.sharding import PartitionSpec as P

HEAD_DIM = 128


def modulate(x_rows, mod):
    whole = lax.all_gather(x_rows, "head", axis=1, tiled=True)
    xf = whole.astype(jnp.float32)
    mean = jnp.mean(xf, axis=1, keepdims=True)
    centered = xf - mean
    var = jnp.mean(centered * centered, axis=1, keepdims=True)
    normed = centered * lax.rsqrt(var + 1e-06)
    return (normed * (1.0 + mod[1]) + mod[0]).astype(jnp.bfloat16)


def attend_block(x_full, keep_full, qkv_weight, out_weight, mod, gains):
    rows, quarter = x_full.shape
    width = qkv_weight.shape[2]
    group = width // HEAD_DIM
    moded = modulate(x_full, mod)
    qkv = jnp.einsum(
        "rd,dsc->rsc",
        moded,
        lax.all_gather(qkv_weight, "branch", axis=0, tiled=True),
        preferred_element_type=jnp.float32,
    )
    qpart = qkv[:, 0].reshape(rows, group, HEAD_DIM)
    kpart = qkv[:, 1].reshape(rows, group, HEAD_DIM)
    query = (
        qpart * lax.rsqrt(jnp.mean(qpart * qpart, axis=2, keepdims=True) + 1e-06) * gains[0]
    ).astype(jnp.bfloat16)
    key = (
        kpart * lax.rsqrt(jnp.mean(kpart * kpart, axis=2, keepdims=True) + 1e-06) * gains[1]
    ).astype(jnp.bfloat16)
    key = key.reshape(rows, width)
    value = qkv[:, 2].astype(jnp.bfloat16)
    scale = 1.0 / HEAD_DIM**0.5
    keep_wire = keep_full.astype(jnp.bfloat16)
    peak = jnp.full((group, rows), -1e30, jnp.float32)
    key_piece = lax.all_gather(key, "seq", axis=0, tiled=True)
    value_piece = lax.all_gather(value, "seq", axis=0, tiled=True)
    keep_piece = lax.all_gather(keep_wire, "seq", axis=0, tiled=True)
    length = key_piece.shape[0]
    key_heads = key_piece.reshape(length, group, HEAD_DIM)
    value_heads = value_piece.reshape(length, group, HEAD_DIM)
    scores = (
        jnp.einsum("rhd,nhd->hrn", query, key_heads, preferred_element_type=jnp.float32) * scale
    )
    valid = keep_piece[None, None, :] > 0.5
    scores = jnp.where(valid, scores, -1e30)
    new_peak = jnp.maximum(peak, jnp.max(scores, axis=2))
    weights = jnp.where(valid, jnp.exp(scores - new_peak[:, :, None]), 0.0)
    total = jnp.sum(weights, axis=2)
    mixed = jnp.einsum(
        "hrn,nhd->hrd",
        weights.astype(jnp.bfloat16),
        value_heads,
        preferred_element_type=jnp.float32,
    )
    attended = (mixed / total[:, :, None]).astype(jnp.bfloat16)
    attended = attended.transpose(1, 0, 2).reshape(rows, width)
    projected = jnp.dot(
        attended,
        lax.all_gather(out_weight, "branch", axis=1, tiled=True),
        preferred_element_type=jnp.float32,
    )
    mine = lax.psum_scatter(projected, "head", scatter_dimension=1, tiled=True)
    gate = lax.dynamic_slice_in_dim(mod[2], lax.axis_index("head") * quarter, quarter, 0)
    return (x_full.astype(jnp.float32) + gate[None, :] * mine).astype(jnp.bfloat16)


def full_block(x_full, keep_full, qkv_weight, out_weight, mod, gains):
    updated = attend_block(x_full, keep_full, qkv_weight, out_weight, mod, gains)
    return updated


def per_device(
    tokens, valid_counts, shared_qkv, shared_out, skipped_qkv, skipped_out, modulation, qk_gains
):
    rows = tokens.shape[0]
    positions = jnp.arange(rows, dtype=jnp.int32)
    keep_all = (positions < valid_counts[0]).astype(jnp.float32)
    forked = full_block(tokens, keep_all, shared_qkv, shared_out, modulation[0], qk_gains[0])
    strong = full_block(forked, keep_all, skipped_qkv, skipped_out, modulation[1], qk_gains[1])
    result = jnp.where(lax.axis_index("branch") == 0, strong, forked)
    return result[None]


def solution(mesh):
    in_specs = (
        P("seq", "head"),
        P("seq"),
        P("branch", None, "head"),
        P("head", "branch"),
        P("branch", None, "head"),
        P("head", "branch"),
        P(),
        P(),
    )
    out_specs = P("branch", "seq", "head")
    return jax.shard_map(
        per_device, mesh=mesh, in_specs=in_specs, out_specs=out_specs, check_vma=False
    )
```

profile of v0, /device:TPU:0, one launch (start us, length us, event | category | flops | bytes accessed | tf_op | source)
XLA Modules:
  0.0 313.8 jit_solution(11347913517500845164)
XLA Ops:
  6.5 0.7 all-gather.10.cloned.1.call-update
  7.3 0.7 all-gather.12.cloned.1.call-update
  8.1 0.7 all-gather.14.cloned.1.call-update
  9.6 12.7 %all-gather.2 = bf16[4,1,256]{2,1,0:T(2,128)(2,1)S(1)} all-gather(bf16[1,1,256]{2,1,0:T(2,128)(2,1)S(1)} %reshape.146), channel_id=1, replica_groups=mesh['branch'=2,'seq'=4,'head'=4] {'seq'}, dimensions={0}, use_global_device_ids=true | all-gather | bytes 2560 | tf_op jit(solution)/shard_map/all_gather | solution.py:45
  22.3 20.5 %all-gather.10.cloned.1.call-done = bf16[256,3072]{1,0:T(8,128)(2,1)} async-done(((bf16[256,768]{1,0:T(8,128)(2,1)}), bf16[256,3072]{1,0:T(8,128)(2,1)}) %all-gather.10.cloned.1.call-update) | async-done | bytes 1572880 | tf_op jit(solution)/shard_map/all_gather | solution.py:10
  42.8 1.8 convert_reduce_fusion.1
  44.6 2.0 fusion.8
  46.6 15.7 %all-gather.12.cloned.1.call-done = bf16[3072,3,384]{2,0,1:T(8,128)(2,1)} async-done(((bf16[1536,3,384]{2,0,1:T(8,128)(2,1)}), bf16[3072,3,384]{2,0,1:T(8,128)(2,1)}) %all-gather.12.cloned.1.call-update) | async-done | bytes 7077904 | tf_op jit(solution)/shard_map/all_gather | solution.py:27
  62.3 5.3 %fusion.19 = f32[256,3,384]{2,0,1:T(8,128)S(1)} fusion(bf16[3072,3,384]{2,0,1:T(8,128)(2,1)} %all-gather.12.cloned.1.call-done, bf16[256,3072]{1,0:T(8,128)(2,1)S(1)} %copy-done, f32[3072]{0:T(1024)S(1)} %bitcast.90, f32[3072]{0:T(1024)S(1)} %bitcast.91, f32[256]{0:T(256)S(1)} %add_rsqrt_fusion.5, f32[256]{0:T(256)S(1)} %broadcast_multiply_fusion.1), kind=kOutput, calls=%fused_computation.27 | convolution fusion | flops 1816657920 | bytes 9857024 | tf_op jit(solution)/shard_map/rd,dsc->rsc/dot_general | solution.py:24
  68.1 19.8 %all_gather.37 = bf16[1024,384]{1,0:T(8,128)(2,1)S(1)} all-gather(bf16[256,384]{1,0:T(8,128)(2,1)S(1)} %fusion.61), channel_id=1, replica_groups=mesh['branch'=2,'seq'=4,'head'=4] {'seq'}, dimensions={0}, use_global_device_ids=true | all-gather | bytes 983040 | tf_op jit(solution)/shard_map/all_gather | solution.py:43
  88.4 18.0 %all-gather = bf16[1024,1,384]{2,0,1:T(8,128)(2,1)S(1)} all-gather(bf16[256,1,384]{2,0,1:T(8,128)(2,1)S(1)} %slice.109), channel_id=2, replica_groups=mesh['branch'=2,'seq'=4,'head'=4] {'seq'}, dimensions={0}, use_global_device_ids=true | all-gather | bytes 983040 | tf_op jit(solution)/shard_map/all_gather | solution.py:44
  106.8 0.8 fusion.12
  107.6 0.9 fusion.14
  108.5 0.9 fusion.53
  109.5 4.4 %fusion.78 = f32[256,3072]{1,0:T(8,128)} fusion(bf16[256,384]{0,1:T(8,128)(2,1)S(1)} %bitcast.87, bf16[384,3072]{1,0:T(8,128)(2,1)} %all-gather.14.cloned.1.call-done), kind=kOutput, calls=%fused_computation.104 | convolution fusion | flops 603979776 | bytes 5701632 | tf_op jit(solution)/shard_map/dot_general | solution.py:65
  114.0 43.3 %reduce-scatter.3.cloned.1.call-done = f32[256,768]{1,0:T(8,128)} async-done(((f32[256,3072]{1,0:T(8,128)}), f32[256,768]{1,0:T(8,128)}) %reduce-scatter.3.cloned.1.call-update) | async-done | bytes 786448 | tf_op jit(solution)/shard_map/reduce_scatter | solution.py:70
  157.3 2.0 add_convert_fusion.1
  159.4 0.5 all-gather.18.cloned.1.call-update
  159.9 0.7 all-gather.20.cloned.1.call-update
  160.7 29.6 %all-gather.16.cloned.1.call-done = bf16[256,3072]{1,0:T(8,128)(2,1)} async-done(((bf16[256,768]{1,0:T(8,128)(2,1)}), bf16[256,3072]{1,0:T(8,128)(2,1)}) %all-gather.16.cloned.1.call-update) | async-done | bytes 1572880 | tf_op jit(solution)/shard_map/all_gather | solution.py:10
  190.3 1.8 convert_reduce_fusion
  192.2 2.0 fusion.4
  194.1 15.5 %all-gather.18.cloned.1.call-done = bf16[3072,3,384]{2,0,1:T(8,128)(2,1)} async-done(((bf16[1536,3,384]{2,0,1:T(8,128)(2,1)}), bf16[3072,3,384]{2,0,1:T(8,128)(2,1)}) %all-gather.18.cloned.1.call-update) | async-done | bytes 7077904 | tf_op jit(solution)/shard_map/all_gather | solution.py:27
  209.7 5.3 %fusion.22 = f32[256,3,384]{2,0,1:T(8,128)S(1)} fusion(bf16[3072,3,384]{2,0,1:T(8,128)(2,1)} %all-gather.18.cloned.1.call-done, bf16[256,3072]{1,0:T(8,128)(2,1)S(1)} %copy-done.1, f32[3072]{0:T(1024)S(1)} %bitcast.88, f32[3072]{0:T(1024)S(1)} %bitcast.89, f32[256]{0:T(256)S(1)} %add_rsqrt_fusion.4, f32[256]{0:T(256)S(1)} %broadcast_multiply_fusion), kind=kOutput, calls=%fused_computation.29 | convolution fusion | flops 1816657920 | bytes 9857024 | tf_op jit(solution)/shard_map/rd,dsc->rsc/dot_general | solution.py:24
  215.5 19.8 %all_gather.42 = bf16[1024,384]{1,0:T(8,128)(2,1)S(1)} all-gather(bf16[256,384]{1,0:T(8,128)(2,1)S(1)} %fusion.59), channel_id=1, replica_groups=mesh['branch'=2,'seq'=4,'head'=4] {'seq'}, dimensions={0}, use_global_device_ids=true | all-gather | bytes 983040 | tf_op jit(solution)/shard_map/all_gather | solution.py:43
  235.8 18.2 %all-gather.1 = bf16[1024,1,384]{2,0,1:T(8,128)(2,1)S(1)} all-gather(bf16[256,1,384]{2,0,1:T(8,128)(2,1)S(1)} %slice.108), channel_id=3, replica_groups=mesh['branch'=2,'seq'=4,'head'=4] {'seq'}, dimensions={0}, use_global_device_ids=true | all-gather | bytes 983040 | tf_op jit(solution)/shard_map/all_gather | solution.py:44
  254.4 0.8 fusion.13
  255.2 0.9 fusion.16
  256.1 0.9 fusion.47
  257.1 4.4 %fusion.79 = f32[256,3072]{1,0:T(8,128)} fusion(bf16[256,384]{0,1:T(8,128)(2,1)S(1)} %bitcast.86, bf16[384,3072]{1,0:T(8,128)(2,1)} %all-gather.20.cloned.1.call-done), kind=kOutput, calls=%fused_computation.105 | convolution fusion | flops 603979776 | bytes 5701632 | tf_op jit(solution)/shard_map/dot_general | solution.py:65
  261.5 43.4 %reduce-scatter.5.cloned.1.call-done = f32[256,768]{1,0:T(8,128)} async-done(((f32[256,3072]{1,0:T(8,128)}), f32[256,768]{1,0:T(8,128)}) %reduce-scatter.5.cloned.1.call-update) | async-done | bytes 786448 | tf_op jit(solution)/shard_map/reduce_scatter | solution.py:70
  304.9 2.0 fusion.57
  (67 shorter events, 3.2 us)
Async XLA Ops:
  6.5 2.3 copy-start.4
  6.5 2.3 copy-start.5
  6.5 36.2 %all-gather.10.cloned.1.call-start = ((), (), s32[]{:S(2)}) async-start(), calls=%async_computation.2 | async-start | bytes 1966080 | tf_op jit(solution)/shard_map/all_gather | solution.py:10
  7.3 55.0 %all-gather.12.cloned.1.call-start = ((), (), s32[]{:S(2)}) async-start(), calls=%async_computation.3 | async-start | bytes 10616832 | tf_op jit(solution)/shard_map/all_gather | solution.py:27
  8.0 101.5 %all-gather.14.cloned.1.call-start = ((), (), s32[]{:S(2)}) async-start(), calls=%async_computation.4 | async-start | bytes 3538944 | tf_op jit(solution)/shard_map/all_gather | solution.py:67
  8.7 148.6 %reduce-scatter.3.cloned.1.call-start = ((), (), s32[]{:S(2)}) async-start(), calls=%async_computation.5 | async-start | bytes 3932160 | tf_op jit(solution)/shard_map/reduce_scatter | solution.py:70
  42.8 19.5 %copy-start = (bf16[256,3072]{1,0:T(8,128)(2,1)S(1)}, bf16[256,3072]{1,0:T(8,128)(2,1)}, u32[]{:S(2)}) copy-start(bf16[256,3072]{1,0:T(8,128)(2,1)} %all-gather.10.cloned.1.call-done) | copy-start | bytes 4718596
  109.5 47.8 %copy-start.3 = (bf16[256,768]{1,0:T(8,128)(2,1)S(1)}, bf16[256,768]{1,0:T(8,128)(2,1)}, u32[]{:S(2)}) copy-start(bf16[256,768]{1,0:T(8,128)(2,1)} %param.8) | copy-start | bytes 1179652
  113.9 76.4 %all-gather.16.cloned.1.call-start = ((), (), s32[]{:S(2)}) async-start(), calls=%async_computation.6 | async-start | bytes 1966080 | tf_op jit(solution)/shard_map/all_gather | solution.py:10
  159.3 50.4 %all-gather.18.cloned.1.call-start = ((), (), s32[]{:S(2)}) async-start(), calls=%async_computation.7 | async-start | bytes 10616832 | tf_op jit(solution)/shard_map/all_gather | solution.py:27
  159.9 97.1 %all-gather.20.cloned.1.call-start = ((), (), s32[]{:S(2)}) async-start(), calls=%async_computation.8 | async-start | bytes 3538944 | tf_op jit(solution)/shard_map/all_gather | solution.py:67
  160.6 144.3 %reduce-scatter.5.cloned.1.call-start = ((), (), s32[]{:S(2)}) async-start(), calls=%async_computation.9 | async-start | bytes 3932160 | tf_op jit(solution)/shard_map/reduce_scatter | solution.py:70
  190.3 19.3 %copy-start.1 = (bf16[256,3072]{1,0:T(8,128)(2,1)S(1)}, bf16[256,3072]{1,0:T(8,128)(2,1)}, u32[]{:S(2)}) copy-start(bf16[256,3072]{1,0:T(8,128)(2,1)} %all-gather.16.cloned.1.call-done) | copy-start | bytes 4718596
  257.0 47.9 %copy-start.2 = (bf16[256,768]{1,0:T(8,128)(2,1)S(1)}, bf16[256,768]{1,0:T(8,128)(2,1)}, u32[]{:S(2)}) copy-start(bf16[256,768]{1,0:T(8,128)(2,1)} %add_convert_fusion.1) | copy-start | bytes 1179652
Sparse Core Ops, SparseCore 0:
  9.2 33.5 all-gather.9
  44.3 17.9 all-gather.11
  63.8 12.1 all-gather.13
  114.0 43.2 reduce-scatter.2
  159.4 30.8 all-gather.15
  191.7 17.9 all-gather.17
  211.2 12.1 all-gather.19
  261.6 43.2 reduce-scatter.4
where the time goes:
time: 314 us
  waiting for transfers between devices  172 us (55%)
  blocking collectives  88.5 us (28%)
  matrix products  22.8 us (7%)
  between operations  14.5 us (5%)
  other arithmetic  13.9 us (4%)
    reduce_scatter x2, waiting for transfers between devices, attend_block(): mine = lax.psum_scatter(projected, 'head', scatter_dimension=1, tiled=True)  86.7 us
    all_gather x2, waiting for transfers between devices, modulate(): whole = lax.all_gather(x_rows, 'head', axis=1, tiled=True)  50.1 us
    all_gather x2, blocking collectives, attend_block(): key_piece = lax.all_gather(key, 'seq', axis=0, tiled=True)  39.7 us
    all_gather x2, blocking collectives, attend_block(): value_piece = lax.all_gather(value, 'seq', axis=0, tiled=True)  36.2 us
    all_gather x2, waiting for transfers between devices, attend_block(): lax.all_gather(qkv_weight, 'branch', axis=0, tiled=True)  31.2 us
    all_gather x1, blocking collectives, attend_block(): keep_piece = lax.all_gather(keep_wire, 'seq', axis=0, tiled=True)  12.7 us
    dot_general x2, matrix products, attend_block(): jnp.einsum('rd,dsc->rsc', moded, lax.all_gather(qkv_weight, 'branch', axi...  10.5 us
    dot_general x2, matrix products, attend_block(): jnp.dot(attended, lax.all_gather(out_weight, 'branch', axis=1, tiled=True...  8.77 us
  transfers between devices with their start and end apart: 8, of which 6 were waited for; matrix products, arithmetic and copies ran while one was open for 8% of the time, Pallas kernels for 0%

commit v1 on v0

--- a/solution.py
+++ b/solution.py
@@ -6,8 +6,29 @@
 HEAD_DIM = 128
 
 
+def finish_files_all(inputs, array_dim):
+    now = list(inputs.shape[1:])
+    now[array_dim] *= inputs.shape[0]
+    return jnp.moveaxis(inputs, 0, array_dim).reshape(now)
+
+
+def wrap_the_goods(raw, row_axis):
+    field_out, opened = (lax.psum(1, row_axis), lax.axis_index(row_axis))
+    part_next, v1 = (raw[None], 1)
+    while v1 < field_out:
+        next_value = lax.ppermute(
+            part_next, row_axis, list(map(lambda idx: (idx, idx ^ v1), range(field_out)))
+        )
+        kept_arr = opened & v1 == 0
+        part_next = jnp.concatenate(
+            [jnp.where(kept_arr, part_next, next_value), jnp.where(kept_arr, next_value, part_next)]
+        )
+        v1 *= 2
+    return part_next
+
+
 def modulate(x_rows, mod):
-    whole = lax.all_gather(x_rows, "head", axis=1, tiled=True)
+    whole = finish_files_all(wrap_the_goods(x_rows, "head"), 1)
     xf = whole.astype(jnp.float32)
     mean = jnp.mean(xf, axis=1, keepdims=True)
     centered = xf - mean

time: 314 us -> 278 us (0.89)
  waiting for transfers between devices: 172 us -> 125 us
  starting transfers between devices: 0.28 us -> 7.99 us
  local copies, waits for them, and re-layouts: 2.33 us -> 9.4 us
  blocking collectives: 88.5 us -> 82.3 us
    all_gather x2 -> x0, waiting for transfers between devices: 50.1 us -> none  [modulate(): whole = lax.all_gather(x_rows, 'head', axis=1, tiled=True)]
    ppermute x0 -> x4, waiting for transfers between devices: none -> 39.9 us  [wrap_the_goods(): lax.ppermute(part_next, row_axis, list(map(lambda idx: (idx, idx ^ v1), r...]
    all_gather x2, waiting for transfers between devices: 31.2 us -> 0.04 us  [attend_block(): lax.all_gather(qkv_weight, 'branch', axis=0, tiled=True)]
    ppermute x0 -> x4, starting transfers between devices: none -> 7.61 us  [wrap_the_goods(): lax.ppermute(part_next, row_axis, list(map(lambda idx: (idx, idx ^ v1), r...]
    convert_element_type x0 -> x4, other arithmetic: none -> 7.3 us  [the longest x2 6.89 us: modulate(): return (normed * (1.0 + mod[1]) + mod[0]).astype(jnp.bfloat16)]
    convert_element_type x0 -> x2, local copies, waits for them, and re-layouts: none -> 4.8 us  [modulate(): xf = whole.astype(jnp.float32)]
    all_gather x2, blocking collectives: 39.7 us -> 36.3 us  [attend_block(): key_piece = lax.all_gather(key, 'seq', axis=0, tiled=True)]
    reduce_scatter x2, waiting for transfers between devices: 86.7 us -> 83.5 us  [attend_block(): mine = lax.psum_scatter(projected, 'head', scatter_dimension=1, tiled=True)]
  transfers between devices with their start and end apart: 8 -> 10, of which waited for: 6 -> 5; matrix products, arithmetic and copies ran while one was open for 8% -> 13% of each run, Pallas kernels for 0% -> 0%
where the time goes in v1:
time: 278 us
  waiting for transfers between devices  125 us (45%)
  blocking collectives  82.3 us (30%)
  matrix products  22.7 us (8%)
  other arithmetic  16.2 us (6%)
  between operations  14.5 us (5%)
  local copies, waits for them, and re-layouts  9.4 us (3%)
  starting transfers between devices  7.99 us (3%)
    reduce_scatter x2, waiting for transfers between devices, attend_block(): mine = lax.psum_scatter(projected, 'head', scatter_dimension=1, tiled=True)  83.5 us
    ppermute x4, waiting for transfers between devices, wrap_the_goods(): lax.ppermute(part_next, row_axis, list(map(lambda idx: (idx, idx ^ v1), r...  39.9 us
    all_gather x2, blocking collectives, attend_block(): key_piece = lax.all_gather(key, 'seq', axis=0, tiled=True)  36.3 us
    all_gather x2, blocking collectives, attend_block(): value_piece = lax.all_gather(value, 'seq', axis=0, tiled=True)  34.8 us
    all_gather x1, blocking collectives, attend_block(): keep_piece = lax.all_gather(keep_wire, 'seq', axis=0, tiled=True)  11.2 us
    dot_general x2, matrix products, attend_block(): jnp.einsum('rd,dsc->rsc', moded, lax.all_gather(qkv_weight, 'branch', axi...  10.5 us
    dot_general x2, matrix products, attend_block(): jnp.dot(attended, lax.all_gather(out_weight, 'branch', axis=1, tiled=True...  8.71 us
    ppermute x4, starting transfers between devices, wrap_the_goods(): lax.ppermute(part_next, row_axis, list(map(lambda idx: (idx, idx ^ v1), r...  7.61 us
  transfers between devices with their start and end apart: 10, of which 5 were waited for; matrix products, arithmetic and copies ran while one was open for 13% of the time, Pallas kernels for 0%

profile of v1, /device:TPU:0, one launch (start us, length us, event | category | flops | bytes accessed | tf_op | source)
XLA Modules:
  0.0 277.8 jit_solution(3893638836795919860)
XLA Ops:
  6.5 0.7 all-gather.8.cloned.1.call-update
  7.5 3.0 %collective-permute-start = (bf16[1,256,768]{2,1,0:T(8,128)(2,1)S(1)}, bf16[1,256,768]{2,1,0:T(8,128)(2,1)S(1)}, u32[]{:S(2)}, u32[]{:S(2)}) collective-permute-start(bf16[1,256,768]{2,1,0:T(8,128)(2,1)S(1)} %bitcast.115), channel_id=1, source_target_pairs={{0,1},{1,0},{2,3},{3,2},{4,5},{5,4},{6,7},{7,6},{8,9},{9,8},{10,11... | collective-permute-start | bytes 1179656 | tf_op jit(solution)/shard_map/ppermute | solution.py:19
  11.2 11.2 %all-gather.2 = bf16[4,1,256]{2,1,0:T(2,128)(2,1)S(1)} all-gather(bf16[1,1,256]{2,1,0:T(2,128)(2,1)S(1)} %reshape.164), channel_id=1, replica_groups=mesh['branch'=2,'seq'=4,'head'=4] {'seq'}, dimensions={0}, use_global_device_ids=true | all-gather | bytes 2560 | tf_op jit(solution)/shard_map/all_gather | solution.py:66
  23.2 1.6 collective-permute-start.1
  25.5 14.8 %collective-permute-done.1 = bf16[2,256,768]{2,1,0:T(8,128)(2,1)S(1)} collective-permute-done((bf16[2,256,768]{2,1,0:T(8,128)(2,1)S(1)}, bf16[2,256,768]{2,1,0:T(8,128)(2,1)S(1)}, u32[]{:S(2)}, u32[]{:S(2)}) %collective-permute-start.1) | collective-permute-done | bytes 786464 | tf_op jit(solution)/shard_map/ppermute | solution.py:19
  41.4 2.4 copy.35
  43.8 3.1 %fusion.11 = bf16[256,3072]{0,1:T(8,128)(2,1)S(1)} fusion(f32[256,4,768]{0,2,1:T(8,128)} %copy.35, f32[3072]{0:T(1024)S(1)} %bitcast.122, f32[3072]{0:T(1024)S(1)} %bitcast.123, f32[256]{0:T(256)S(1)} %add_rsqrt_fusion.5, f32[256]{0:T(256)S(1)} %broadcast_multiply_fusion.1), kind=kLoop, calls=%fused_computation.19 | loop fusion | flops 3932160 | bytes 4745216 | tf_op jit(solution)/shard_map/convert_element_type | solution.py:37
  46.9 5.2 %fusion.20 = f32[256,3,384]{2,0,1:T(8,128)S(1)} fusion(bf16[3072,3,384]{2,0,1:T(8,128)(2,1)} %all-gather.8.cloned.1.call-done, bf16[256,3072]{0,1:T(8,128)(2,1)S(1)} %fusion.11), kind=kOutput, calls=%fused_computation.34 | convolution fusion | flops 1811939328 | bytes 9830400 | tf_op jit(solution)/shard_map/rd,dsc->rsc/dot_general | solution.py:45
  52.8 17.8 %all_gather.30 = bf16[1024,384]{1,0:T(8,128)(2,1)S(1)} all-gather(bf16[256,384]{1,0:T(8,128)(2,1)S(1)} %fusion.51), channel_id=1, replica_groups=mesh['branch'=2,'seq'=4,'head'=4] {'seq'}, dimensions={0}, use_global_device_ids=true | all-gather | bytes 983040 | tf_op jit(solution)/shard_map/all_gather | solution.py:64
  71.0 17.4 %all-gather = bf16[1024,1,384]{2,0,1:T(8,128)(2,1)S(1)} all-gather(bf16[256,1,384]{2,0,1:T(8,128)(2,1)S(1)} %slice.109), channel_id=2, replica_groups=mesh['branch'=2,'seq'=4,'head'=4] {'seq'}, dimensions={0}, use_global_device_ids=true | all-gather | bytes 983040 | tf_op jit(solution)/shard_map/all_gather | solution.py:65
  88.8 0.8 fusion.12
  89.6 0.9 fusion.14
  90.5 0.9 fusion.43
  91.5 4.4 %fusion.68 = f32[256,3072]{1,0:T(8,128)} fusion(bf16[256,384]{0,1:T(8,128)(2,1)S(1)} %bitcast.119, bf16[384,3072]{1,0:T(8,128)(2,1)} %all-gather.10.cloned.1.call-done), kind=kOutput, calls=%fused_computation.112 | convolution fusion | flops 603979776 | bytes 5701632 | tf_op jit(solution)/shard_map/dot_general | solution.py:86
  96.5 42.1 %reduce-scatter.3.cloned.1.call-done = f32[256,768]{1,0:T(8,128)} async-done(((f32[256,3072]{1,0:T(8,128)}), f32[256,768]{1,0:T(8,128)}) %reduce-scatter.3.cloned.1.call-update) | async-done | bytes 786448 | tf_op jit(solution)/shard_map/reduce_scatter | solution.py:91
  138.7 1.2 add_convert_fusion.1
  139.9 1.5 collective-permute-start.2
  141.4 9.2 %collective-permute-done.2 = bf16[1,256,768]{2,1,0:T(8,128)(2,1)S(1)} collective-permute-done((bf16[1,256,768]{2,1,0:T(8,128)(2,1)S(1)}, bf16[1,256,768]{2,1,0:T(8,128)(2,1)S(1)}, u32[]{:S(2)}, u32[]{:S(2)}) %collective-permute-start.2) | collective-permute-done | bytes 393248 | tf_op jit(solution)/shard_map/ppermute | solution.py:19
  150.8 1.5 collective-permute-start.3
  153.2 15.9 %collective-permute-done.3 = bf16[2,256,768]{2,1,0:T(8,128)(2,1)S(1)} collective-permute-done((bf16[2,256,768]{2,1,0:T(8,128)(2,1)S(1)}, bf16[2,256,768]{2,1,0:T(8,128)(2,1)S(1)}, u32[]{:S(2)}, u32[]{:S(2)}) %collective-permute-start.3) | collective-permute-done | bytes 786464 | tf_op jit(solution)/shard_map/ppermute | solution.py:19
  170.9 2.4 copy.44
  173.3 3.8 %fusion.7 = bf16[256,3072]{0,1:T(8,128)(2,1)S(1)} fusion(f32[256,4,768]{0,2,1:T(8,128)} %copy.44, f32[3072]{0:T(1024)S(1)} %bitcast.120, f32[3072]{0:T(1024)} %bitcast.121, f32[256]{0:T(256)} %add_rsqrt_fusion.4, f32[256]{0:T(256)} %copy-done.3), kind=kLoop, calls=%fused_computation.14 | loop fusion | flops 3932160 | bytes 4745216 | tf_op jit(solution)/shard_map/convert_element_type | solution.py:37
  177.2 5.2 %fusion.18 = f32[256,3,384]{2,0,1:T(8,128)S(1)} fusion(bf16[3072,3,384]{2,0,1:T(8,128)(2,1)} %all-gather.12.cloned.1.call-done, bf16[256,3072]{0,1:T(8,128)(2,1)S(1)} %fusion.7), kind=kOutput, calls=%fused_computation.32 | convolution fusion | flops 1811939328 | bytes 9830400 | tf_op jit(solution)/shard_map/rd,dsc->rsc/dot_general | solution.py:45
  183.2 18.5 %all_gather.34 = bf16[1024,384]{1,0:T(8,128)(2,1)S(1)} all-gather(bf16[256,384]{1,0:T(8,128)(2,1)S(1)} %fusion.49), channel_id=1, replica_groups=mesh['branch'=2,'seq'=4,'head'=4] {'seq'}, dimensions={0}, use_global_device_ids=true | all-gather | bytes 983040 | tf_op jit(solution)/shard_map/all_gather | solution.py:64
  202.1 17.4 %all-gather.1 = bf16[1024,1,384]{2,0,1:T(8,128)(2,1)S(1)} all-gather(bf16[256,1,384]{2,0,1:T(8,128)(2,1)S(1)} %slice.108), channel_id=3, replica_groups=mesh['branch'=2,'seq'=4,'head'=4] {'seq'}, dimensions={0}, use_global_device_ids=true | all-gather | bytes 983040 | tf_op jit(solution)/shard_map/all_gather | solution.py:65
  219.9 0.8 fusion.13
  220.7 0.9 fusion.16
  221.6 0.9 fusion.37
  222.6 4.3 %fusion.69 = f32[256,3072]{1,0:T(8,128)} fusion(bf16[256,384]{0,1:T(8,128)(2,1)S(1)} %bitcast.118, bf16[384,3072]{1,0:T(8,128)(2,1)} %all-gather.14.cloned.1.call-done), kind=kOutput, calls=%fused_computation.113 | convolution fusion | flops 603979776 | bytes 5701632 | tf_op jit(solution)/shard_map/dot_general | solution.py:86
  227.0 0.7 dynamic-slice_reduce_fusion
  227.7 41.3 %reduce-scatter.5.cloned.1.call-done = f32[256,768]{1,0:T(8,128)} async-done(((f32[256,3072]{1,0:T(8,128)}), f32[256,768]{1,0:T(8,128)}) %reduce-scatter.5.cloned.1.call-update) | async-done | bytes 786448 | tf_op jit(solution)/shard_map/reduce_scatter | solution.py:91
  269.0 2.0 fusion.47
  (85 shorter events, 9.3 us)
Async XLA Ops:
  6.5 1.0 copy-start
  6.5 15.9 %copy-start.6 = (f32[2,2,128]{2,1,0:T(2,128)S(1)}, f32[2,2,128]{2,1,0:T(2,128)}, u32[]{:S(2)}) copy-start(f32[2,2,128]{2,1,0:T(2,128)} %param.15) | copy-start | bytes 6148
  6.5 40.4 %all-gather.8.cloned.1.call-start = ((), (), s32[]{:S(2)}) async-start(), calls=%async_computation.2 | async-start | bytes 10616832 | tf_op jit(solution)/shard_map/all_gather | solution.py:48
  6.5 18.2 %copy-start.2 = (f32[2,3,3072]{2,0,1:T(2,128)S(1)}, f32[2,3,3072]{2,0,1:T(2,128)}, u32[]{:S(2)}) copy-start(f32[2,3,3072]{2,0,1:T(2,128)} %param.14) | copy-start | bytes 221188
  7.3 84.2 %all-gather.10.cloned.1.call-start = ((), (), s32[]{:S(2)}) async-start(), calls=%async_computation.3 | async-start | bytes 3538944 | tf_op jit(solution)/shard_map/all_gather | solution.py:88
  7.5 15.5 %collective-permute-start = (bf16[1,256,768]{2,1,0:T(8,128)(2,1)S(1)}, bf16[1,256,768]{2,1,0:T(8,128)(2,1)S(1)}, u32[]{:S(2)}, u32[]{:S(2)}) collective-permute-start(bf16[1,256,768]{2,1,0:T(8,128)(2,1)S(1)} %bitcast.115), channel_id=1, source_target_pairs={{0,1},{1,0},{2,3},{3,2},{4,5},{5,4},{6,7},{7,6},{8,9},{9,8},{10,11... | collective-permute-start | bytes 1179656 | tf_op jit(solution)/shard_map/ppermute | solution.py:19
  10.5 128.2 %reduce-scatter.3.cloned.1.call-start = ((), (), s32[]{:S(2)}) async-start(), calls=%async_computation.4 | async-start | bytes 3932160 | tf_op jit(solution)/shard_map/reduce_scatter | solution.py:91
  23.2 17.0 %collective-permute-start.1 = (bf16[2,256,768]{2,1,0:T(8,128)(2,1)S(1)}, bf16[2,256,768]{2,1,0:T(8,128)(2,1)S(1)}, u32[]{:S(2)}, u32[]{:S(2)}) collective-permute-start(bf16[2,256,768]{2,1,0:T(8,128)(2,1)S(1)} %pad_maximum_fusion.2), channel_id=1, source_target_pairs={{0,2},{1,3},{2,0},{3,1},{4,6},{5,7},{6,4},{7,5},{8,10},{9,11},{10,... | collective-permute-start | bytes 2359304 | tf_op jit(solution)/shard_map/ppermute | solution.py:19
  95.9 42.8 %copy-start.1 = (bf16[256,768]{1,0:T(8,128)(2,1)S(1)}, bf16[256,768]{1,0:T(8,128)(2,1)}, u32[]{:S(2)}) copy-start(bf16[256,768]{1,0:T(8,128)(2,1)} %param.8) | copy-start | bytes 1179652
  95.9 81.3 %all-gather.12.cloned.1.call-start = ((), (), s32[]{:S(2)}) async-start(), calls=%async_computation.5 | async-start | bytes 10616832 | tf_op jit(solution)/shard_map/all_gather | solution.py:48
  96.5 56.1 %copy-start.7 = (f32[128]{0:T(128)S(1)}, f32[128]{0:T(128)}, u32[]{:S(2)}) copy-start(f32[128]{0:T(128)} %get-tuple-element.26) | copy-start | bytes 1540
  96.5 126.1 %all-gather.14.cloned.1.call-start = ((), (), s32[]{:S(2)}) async-start(), calls=%async_computation.6 | async-start | bytes 3538944 | tf_op jit(solution)/shard_map/all_gather | solution.py:88
  139.9 10.7 %collective-permute-start.2 = (bf16[1,256,768]{2,1,0:T(8,128)(2,1)S(1)}, bf16[1,256,768]{2,1,0:T(8,128)(2,1)S(1)}, u32[]{:S(2)}, u32[]{:S(2)}) collective-permute-start(bf16[1,256,768]{2,1,0:T(8,128)(2,1)S(1)} %bitcast.108), channel_id=1, source_target_pairs={{0,1},{1,0},{2,3},{3,2},{4,5},{5,4},{6,7},{7,6},{8,9},{9,8},{10,11... | collective-permute-start | bytes 1179656 | tf_op jit(solution)/shard_map/ppermute | solution.py:19
  150.8 18.3 %collective-permute-start.3 = (bf16[2,256,768]{2,1,0:T(8,128)(2,1)S(1)}, bf16[2,256,768]{2,1,0:T(8,128)(2,1)S(1)}, u32[]{:S(2)}, u32[]{:S(2)}) collective-permute-start(bf16[2,256,768]{2,1,0:T(8,128)(2,1)S(1)} %pad_maximum_fusion.3), channel_id=1, source_target_pairs={{0,2},{1,3},{2,0},{3,1},{4,6},{5,7},{6,4},{7,5},{8,10},{9,11},{10,... | collective-permute-start | bytes 2359304 | tf_op jit(solution)/shard_map/ppermute | solution.py:19
  152.3 116.7 %reduce-scatter.5.cloned.1.call-start = ((), (), s32[]{:S(2)}) async-start(), calls=%async_computation.7 | async-start | bytes 3932160 | tf_op jit(solution)/shard_map/reduce_scatter | solution.py:91
  169.7 0.6 copy-start.3
  182.4 0.7 copy-start.4
  183.2 36.7 %copy-start.5 = (f32[128]{0:T(128)S(1)}, f32[128]{0:T(128)}, u32[]{:S(2)}) copy-start(f32[128]{0:T(128)} %get-tuple-element.23) | copy-start | bytes 1540
Sparse Core Ops, SparseCore 0:
  8.9 20.6 all-gather.7
  31.1 12.1 all-gather.9
  96.0 42.6 reduce-scatter.2
  140.1 17.8 all-gather.11
  159.4 12.1 all-gather.13
  227.1 41.8 reduce-scatter.4
